TPU v7x, 128 devices: a whole 4x4x4 slice. The times are simulated.
128 devices in a mesh: kring: 8 (over y, x_lo), band: 16 (over z, x_hi, core).
Axes of the slice: x: 4 (x_hi: 2, x_lo: 2; x = x_hi * 2 + x_lo), y: 4, z: 4, core: 2. Of those that a mesh axis runs over, the one named last changes fastest.
Arguments:
- current: bfloat16 [262144, 256], P(('kring', 'band')), may hold values from -61 to 61
- previous: bfloat16 [262144, 256], P(('kring', 'band')), may hold values from -6 to 6
- energies: float32 [262144], P(('kring', 'band')), may hold values from 1.5 to 2.5
- targets: int32 [262144], P(('kring', 'band')), may hold values from 0 to 15, as said below
- layer_ids: int32 [327680], P(('kring', 'band')), may hold values from 0 to 1
- conduction_pairs: bfloat16 [327680, 1024], P(('kring', 'band')), may hold values from -0.375 to 0.375
- valence_pairs: bfloat16 [327680, 1024], P(('kring', 'band')), may hold values from -0.228125 to 0.228125
- exchange_pairs: bfloat16 [327680, 1024], P(('kring', 'band')), may hold values from -0.137001939 to 0.137001939
- screened: bfloat16 [8, 2, 1024, 2, 1024], P(None, None, 'band'), may hold values from -0.03203125 to 1.28203125
- coulomb: float32 [2, 2, 1024], replicated, may hold values from 0.2 to 2
- beta_prev: float32 [256], replicated, may hold values from 0.5 to 2
Outputs:
- next_vector: bfloat16 [262144, 256], P(('kring', 'band'))
- lanczos_alpha: float32 [256], replicated
- lanczos_beta: float32 [256], replicated
Inputs may be any that keep to these rules, and one draw needn't show every extreme that they name: `targets`: the 2048 rows of one device name each band index at most 2560 // 16 times; in every k-group one band index is named exactly that often by every device of the group.
All inputs are finite; a program needn't handle non-finite values.
Results may differ from a plain program's by a relative error of at most 0.0057.
Values may be sent and summed in bfloat16 or wider, within the bound.
A program may use at most 128 MiB of HBM per device.

v0:
```python
import jax
import jax.numpy as jnp
from jax import lax
from jax.sharding import PartitionSpec as P

epsilon_mean = 1e-06


def place_rows(targets, capacity, band_count):
    onehot = (targets[:, None] == jnp.arange(band_count, dtype=jnp.int32)[None, :]).astype(
        jnp.int32
    )
    counted = jnp.cumsum(onehot, axis=0)
    ranking = jnp.sum(counted * onehot, axis=1) - 1
    return targets * capacity + ranking


def per_device(
    current,
    previous,
    energies,
    targets,
    layer_ids,
    conduction_pairs,
    valence_pairs,
    exchange_pairs,
    screened,
    coulomb,
    beta_prev,
):
    band_count = lax.axis_size("band")
    own_rows, chains = current.shape
    slot_rows, basis_size = conduction_pairs.shape
    capacity = slot_rows // band_count
    slot_ids = place_rows(targets, capacity, band_count)
    outgoing = jnp.zeros((slot_rows, chains), jnp.bfloat16).at[slot_ids].set(current)
    arrived = lax.all_to_all(
        outgoing.reshape(band_count, capacity, chains),
        "band",
        split_axis=0,
        concat_axis=0,
        tiled=True,
    ).reshape(slot_rows, chains)
    layer_pick = (layer_ids[:, None] == jnp.arange(2, dtype=jnp.int32)[None, :]).astype(
        jnp.bfloat16
    )
    split_amps = arrived[:, None, :] * layer_pick[:, :, None]
    valence_part = jnp.einsum(
        "tg,tln->lgn", valence_pairs, split_amps, preferred_element_type=jnp.float32
    )
    exchange_part = jnp.einsum(
        "tg,tln->lgn", exchange_pairs, split_amps, preferred_element_type=jnp.float32
    )
    projected = lax.psum_scatter(valence_part, "band", scatter_dimension=1, tiled=True).astype(
        jnp.bfloat16
    )
    exchange_total = lax.psum(exchange_part, ("kring", "band"))
    coupled = (
        coulomb[:, 0, :, None] * exchange_total[0][None]
        + coulomb[:, 1, :, None] * exchange_total[1][None]
    ).astype(jnp.bfloat16)
    group_index = lax.axis_index("kring")
    group_count = lax.axis_size("kring")
    pieces = lax.all_gather(projected[None], "kring", axis=0, tiled=True)
    number = pieces.shape[0]
    distance = jnp.mod(group_index - jnp.arange(number, dtype=jnp.int32), group_count)
    blocks = jnp.take(screened, distance, axis=0)
    direct_part = jnp.einsum("kaphg,kapn->hgn", blocks, pieces, preferred_element_type=jnp.float32)
    direct = lax.psum(direct_part, "band").astype(jnp.bfloat16)
    both_direct = jnp.einsum(
        "tg,lgn->tln", conduction_pairs, direct, preferred_element_type=jnp.float32
    )
    both_exchange = jnp.einsum(
        "tg,lgn->tln", exchange_pairs, coupled, preferred_element_type=jnp.float32
    )
    kernel_all = 2.0 * both_exchange - both_direct
    kernel_rows = jnp.sum(kernel_all * layer_pick.astype(jnp.float32)[:, :, None], axis=1).astype(
        jnp.bfloat16
    )
    returned = lax.all_to_all(
        kernel_rows.reshape(band_count, capacity, chains),
        "band",
        split_axis=0,
        concat_axis=0,
        tiled=True,
    ).reshape(slot_rows, chains)
    kernel_own = returned[slot_ids].astype(jnp.float32)
    current_wide = current.astype(jnp.float32)
    applied = energies[:, None] * current_wide + kernel_own
    start_vec = applied - beta_prev[None, :] * previous.astype(jnp.float32)
    total_rows = own_rows * group_count * band_count
    projection, self_norm = lax.psum(
        (jnp.sum(current_wide * start_vec, axis=0), jnp.sum(current_wide * current_wide, axis=0)),
        ("kring", "band"),
    )
    lanczos_alpha = projection / self_norm
    residual = start_vec - lanczos_alpha[None, :] * current_wide
    residual_sq = lax.psum(jnp.sum(residual * residual, axis=0), ("kring", "band"))
    lanczos_beta = jnp.sqrt(residual_sq / total_rows + epsilon_mean)
    next_vector = (residual / lanczos_beta[None, :]).astype(jnp.bfloat16)
    return (next_vector, lanczos_alpha, lanczos_beta)


def solution(mesh):
    in_specs = (
        P(("kring", "band"), None),
        P(("kring", "band"), None),
        P(("kring", "band")),
        P(("kring", "band")),
        P(("kring", "band")),
        P(("kring", "band"), None),
        P(("kring", "band"), None),
        P(("kring", "band"), None),
        P(None, None, "band", None, None),
        P(),
        P(),
    )
    out_specs = (P(("kring", "band"), None), P(), P())
    return jax.shard_map(
        per_device, mesh=mesh, in_specs=in_specs, out_specs=out_specs, check_vma=False
    )
```

profile of v0, /device:TPU:1, one launch (start us, length us, event | category | flops | bytes accessed | tf_op | source)
XLA Modules:
  0.0 529.2 jit_solution(18126593749929816699)
XLA Ops:
  7.2 0.7 fusion.48
  7.9 4.5 reduce-window.6
  12.4 0.4 slice_reduce_fusion
  12.9 0.2 reduce-window.9
  13.0 0.1 broadcast_add_fusion
  13.1 0.0 copy-start.4
  13.2 0.0 copy-start.3
  13.2 0.0 copy-start.8
  13.2 0.8 fusion.47
  13.9 0.7 broadcast_clamp_fusion
  14.7 10.8 %scatter_custom_fusion = bf16[2560,256]{1,0:T(8,128)(2,1)} fusion(s32[2048]{0:T(1024)S(1)} %get-tuple-element.8, bf16[2048,256]{1,0:T(8,128)(2,1)} %param.11, bf16[]{:T(256)} %constant.46.clone.1), kind=kCustom, calls=%fused_computation.44 | custom fusion | bytes 1311232 | tf_op jit(solution)/shard_map/scatter | solution.py:36
  25.5 9.3 %all-to-all-start = ((bf16[16,160,256]{2,1,0:T(8,128)(2,1)}), bf16[16,160,256]{2,1,0:T(8,128)(2,1)S(1)}, u32[]{:S(2)}, u32[]{:S(2)}) async-start(bf16[16,160,256]{2,1,0:T(8,128)(2,1)} %bitcast.2), calls=%async_computation | async-start | bytes 2621440 | tf_op jit(solution)/shard_map/all_to_all | solution.py:37
  34.8 0.2 all-reduce.6.cloned.1.call-start
  35.0 0.0 copy-done.4
  35.1 0.0 copy-done.3
  35.1 0.0 copy-done.8
  35.1 0.6 dynamic-slice
  36.4 12.0 %gather_fusion = bf16[8,2,64,2,1024]{4,3,2,1,0:T(2,128)(2,1)} fusion(bf16[8,2,64,2,1024]{4,3,2,1,0:T(2,128)(2,1)} %param.19, s32[1024]{0:T(1024)S(1)} %pad_clamp_fusion), kind=kCustom, calls=%fused_computation | custom fusion | bytes 8388640 | tf_op jit(solution)/shard_map/jit(_take)/gather | solution.py:67
  48.4 7.8 %broadcast_select_fusion = bf16[8,2,64,2,1024]{4,3,2,1,0:T(2,128)(2,1)} fusion(bf16[8,2,64,2,1024]{4,3,2,1,0:T(2,128)(2,1)} %gather_fusion, pred[8]{0:T(512)(128)(4,1)S(1)} %compare_and_fusion), kind=kLoop, calls=%fused_computation.3 | loop fusion | flops 2097152 | bytes 8388616 | tf_op jit(solution)/shard_map/jit(_take)/select_n | solution.py:67
  56.2 0.0 all-to-all-done
  56.2 0.8 copy.21
  57.0 6.7 %fusion.28 = f32[2,1024,256]{1,2,0:T(8,128)} fusion(bf16[2560,1024]{1,0:T(8,128)(2,1)} %param.17, bf16[2560,2]{0,1:T(2,128)(2,1)S(1)} %get-tuple-element.10, bf16[2560,256]{0,1:T(8,128)(2,1)S(1)} %copy.21), kind=kOutput, calls=%fused_computation.32 | convolution fusion | flops 2685665280 | bytes 8660992 | tf_op jit(solution)/shard_map/tg,tln->lgn/dot_general | solution.py:48
  63.6 2.8 copy.22
  66.5 84.6 %all-reduce.7 = bf16[2,1024,256]{2,0,1:T(2,128)(2,1)} all-reduce(f32[2,1024,256]{2,0,1:T(2,128)S(1)} %copy.22), channel_id=3, replica_groups=mesh['kring'=8,'band'=16] {'band'}, use_global_device_ids=true, to_apply=%region_5.6.clone | all-reduce | flops 524288 | bytes 3145728
  151.1 0.9 dynamic-slice_convert_fusion
  152.0 0.0 slice-start
  152.0 25.1 %all-gather = bf16[16,64,256]{2,1,0:T(8,128)(2,1)S(1)} all-gather(bf16[2,64,256]{2,1,0:T(8,128)(2,1)S(1)} %copy.23), channel_id=2, replica_groups=mesh['kring'=8,'band'=16] {'kring'}, dimensions={0}, use_global_device_ids=true | all-gather | bytes 589824 | tf_op jit(solution)/shard_map/all_gather | solution.py:64
  177.1 0.0 slice-start.1
  177.1 4.3 fusion.20
  181.4 0.0 slice-done
  181.4 0.0 slice-done.1
  181.4 4.3 fusion.23
  185.7 0.0 all-reduce.6.cloned.1.call-update
  185.7 91.2 %all-reduce.8 = bf16[2,1024,256]{2,1,0:T(8,128)(2,1)S(1)} all-reduce(f32[2,1024,256]{2,1,0:T(8,128)S(1)} %fusion.20), channel_id=1, replica_groups=mesh['kring'=8,'band'=16] {'band'}, use_global_device_ids=true, to_apply=%region_6.7 | all-reduce | flops 524288 | bytes 3145728 | tf_op jit(solution)/shard_map/psum | solution.py:69
  277.0 7.3 %fusion.1 = f32[2,256,2560]{2,1,0:T(8,128)} fusion(bf16[2560,1024]{1,0:T(8,128)(2,1)} %param.16, bf16[2,1024,256]{2,1,0:T(8,128)(2,1)S(1)} %all-reduce.8), kind=kOutput, calls=%fused_computation.6 | convolution fusion | flops 2684354560 | bytes 11534336 | tf_op jit(solution)/shard_map/tg,lgn->tln/dot_general | solution.py:70
  284.3 64.9 %all-reduce.6.cloned.1.call-done = f32[2,1024,256]{1,2,0:T(8,128)} async-done(((f32[2,1024,256]{1,2,0:T(8,128)}), f32[2,1024,256]{1,2,0:T(8,128)}) %all-reduce.6.cloned.1.call-update) | async-done | bytes 2097168 | tf_op jit(solution)/shard_map/psum | solution.py:57
  349.2 1.7 slice_bitcast_fusion.1
  350.9 6.9 %fusion = bf16[2560,256]{0,1:T(8,128)(2,1)S(1)} fusion(f32[2,256,2560]{2,1,0:T(8,128)} %fusion.1, bf16[2560,1024]{1,0:T(8,128)(2,1)} %param.18, f32[2560,2]{0,1:T(2,128)S(1)} %get-tuple-element.9, f32[1024,256]{0,1:T(8,128)S(1)} %get-tuple-element.12, f32[2,1024]{1,0:T(2,128)S(1)} %get-tuple-element.15, f32[1024,256]{0,1:T(8,128)S(1)} %get-tuple-element.11, ...), kind=kOutput, calls=%fused_computation.5 | convolution fusion | flops 2691039232 | bytes 13930496 | tf_op jit(solution)/shard_map/tg,lgn->tln/dot_general | solution.py:73
  357.8 0.6 copy.27
  358.4 25.4 %all_to_all.10 = bf16[16,160,256]{2,1,0:T(8,128)(2,1)S(1)} all-to-all(bf16[16,160,256]{2,1,0:T(8,128)(2,1)S(1)} %bitcast.66), channel_id=1, replica_groups=mesh['kring'=8,'band'=16] {'band'}, dimensions={0} | all-to-all | bytes 2621440 | tf_op jit(solution)/shard_map/all_to_all | solution.py:80
  383.8 0.0 copy-start
  383.8 0.0 copy-start.2
  383.8 0.0 copy-start.5
  383.8 7.5 %gather_fusion.1 = bf16[2048,256]{1,0:T(8,128)(2,1)S(1)} fusion(bf16[2560,256]{1,0:T(8,128)(2,1)S(1)} %bitcast.64, s32[2048]{0:T(1024)S(1)} %get-tuple-element.7), kind=kCustom, calls=%fused_computation.1 | custom fusion | bytes 2105344 | tf_op jit(solution)/shard_map/gather | solution.py:87
  391.3 0.0 copy-done
  391.3 0.0 copy-done.2
  391.3 0.0 copy-done.5
  391.4 0.0 copy-start.1
  391.4 2.1 fusion.18
  393.5 63.6 %all-reduce.1 = (f32[256]{0:T(256)S(1)}, f32[256]{0:T(256)S(1)}) all-reduce(f32[256]{0:T(256)S(1)} %get-tuple-element.4, f32[256]{0:T(256)S(1)} %get-tuple-element.3), channel_id=1, replica_groups=mesh['kring'=8,'band'=16] {'kring','band'}, use_global_device_ids=true, to_apply=%region_9.10 | all-reduce | flops 512 | bytes 4096 | tf_op jit(solution)/shard_map/psum | solution.py:92
  457.1 0.0 copy-done.1
  457.1 0.0 copy-start.6
  457.1 0.8 multiply_reduce_fusion
  457.9 62.7 %psum.39 = f32[256]{0:T(256)S(1)} all-reduce(f32[256]{0:T(256)S(1)} %multiply_reduce_fusion), channel_id=1, replica_groups=mesh['kring'=8,'band'=16] {'kring','band'}, use_global_device_ids=true, to_apply=%region_13.14 | all-reduce | flops 256 | bytes 2048 | tf_op jit(solution)/shard_map/psum | solution.py:98
  520.6 0.0 copy-start.7
  520.6 1.7 divide_convert_fusion
  522.4 0.0 copy-done.6
  522.4 0.0 copy-done.7
  (10 shorter events, 0.1 us)
Async XLA Ops:
  13.1 21.9 %copy-start.4 = (s32[2560]{0:T(1024)S(1)}, s32[2560]{0:T(1024)}, u32[]{:S(2)}) copy-start(s32[2560]{0:T(1024)} %param.15) | copy-start | bytes 30724
  13.2 21.9 %copy-start.3 = (f32[2,2,1024]{2,1,0:T(2,128)S(1)}, f32[2,2,1024]{2,1,0:T(2,128)}, u32[]{:S(2)}) copy-start(f32[2,2,1024]{2,1,0:T(2,128)} %param.20) | copy-start | bytes 49156
  13.2 22.0 %copy-start.8 = (u32[128]{0:T(128)S(1)}, u32[128]{0:T(128)}, u32[]{:S(2)}) copy-start(u32[128]{0:T(128)} %constant.62) | copy-start | bytes 1540
  25.5 30.7 %all-to-all-start = ((bf16[16,160,256]{2,1,0:T(8,128)(2,1)}), bf16[16,160,256]{2,1,0:T(8,128)(2,1)S(1)}, u32[]{:S(2)}, u32[]{:S(2)}) async-start(bf16[16,160,256]{2,1,0:T(8,128)(2,1)} %bitcast.2), calls=%async_computation | async-start | bytes 2621440 | tf_op jit(solution)/shard_map/all_to_all | solution.py:37
  34.8 314.4 %all-reduce.6.cloned.1.call-start = ((), (), s32[]{:S(2)}) async-start(), calls=%async_computation.2 | async-start | bytes 4194304 | tf_op jit(solution)/shard_map/psum | solution.py:57
  152.0 29.4 %slice-start = ((s8[5242880]{0:T(1024)(128)(4,1)}), s8[4194304]{0:T(1024)(128)(4,1)S(1)}, s32[]{:S(2)}) async-start(s8[5242880]{0:T(1024)(128)(4,1)} %bitcast.71), calls=%async_computation.3 | async-start | bytes 8388608
  177.1 4.3 slice-start.1
  383.8 7.5 %copy-start = (bf16[2048,256]{1,0:T(8,128)(2,1)S(1)}, bf16[2048,256]{1,0:T(8,128)(2,1)}, u32[]{:S(2)}) copy-start(bf16[2048,256]{1,0:T(8,128)(2,1)} %param.11) | copy-start | bytes 3145732
  383.8 7.5 %copy-start.2 = (f32[2048]{0:T(1024)S(1)}, f32[2048]{0:T(1024)}, u32[]{:S(2)}) copy-start(f32[2048]{0:T(1024)} %param.13) | copy-start | bytes 24580
  383.8 7.5 %copy-start.5 = (f32[256]{0:T(256)S(1)}, f32[256]{0:T(256)}, u32[]{:S(2)}) copy-start(f32[256]{0:T(256)} %param.21) | copy-start | bytes 3076
  391.4 65.7 %copy-start.1 = (bf16[2048,256]{1,0:T(8,128)(2,1)S(1)}, bf16[2048,256]{1,0:T(8,128)(2,1)}, u32[]{:S(2)}) copy-start(bf16[2048,256]{1,0:T(8,128)(2,1)} %param.12) | copy-start | bytes 3145732
  457.1 65.3 %copy-start.6 = (f32[256]{0:T(256)}, f32[256]{0:T(256)S(1)}, u32[]{:S(2)}) copy-start(f32[256]{0:T(256)S(1)} %div.17) | copy-start | bytes 3076
  520.6 1.8 copy-start.7
Sparse Core Ops, SparseCore 0:
  185.9 163.2 all-reduce.5
where the time goes:
time: 530 us; the launch traced here: 529 us
  blocking collectives  353 us (67%)
  waiting for transfers between devices  64.9 us (12%)
  local copies, waits for them, and re-layouts  38.2 us (7%)
  matrix products  29.5 us (6%)
  other arithmetic  19.5 us (4%)
  between operations  14.9 us (3%)
  starting transfers between devices  9.51 us (2%)
    psum x1, blocking collectives, per_device(): direct = lax.psum(direct_part, 'band').astype(jnp.bfloat16)  91.2 us
    unnamed x1, blocking collectives  84.6 us
    psum x1, waiting for transfers between devices, per_device(): exchange_total = lax.psum(exchange_part, ('kring', 'band'))  64.9 us
    psum x1, blocking collectives, per_device(): lax.psum((jnp.sum(current_wide * start_vec, axis=0), jnp.sum(current_wide...  63.6 us
    psum x1, blocking collectives, per_device(): lax.psum(jnp.sum(residual * residual, axis=0), ('kring', 'band'))  62.7 us
    all_to_all x1, blocking collectives, per_device(): lax.all_to_all(kernel_rows.reshape(band_count, capacity, chains), 'band',...  25.4 us
    all_gather x1, blocking collectives, per_device(): pieces = lax.all_gather(projected[None], 'kring', axis=0, tiled=True)  25.1 us
    gather x1, local copies, waits for them, and re-layouts, per_device(): blocks = jnp.take(screened, distance, axis=0)  12 us
  transfers between devices with their start and end apart: 2, of which 1 were waited for; matrix products, arithmetic and copies ran while one was open for 5% of the time, Pallas kernels for 0%

commit v1 on v0

v1 whole, which is shorter than its diff:
```python
import functools

import jax
import jax.numpy as jnp
from jax import lax
from jax.experimental import pallas as pl
from jax.experimental.pallas import tpu as pltpu
from jax.sharding import PartitionSpec as P

MESH = pl.DeviceIdType.MESH
F32 = jnp.float32
BF16 = jnp.bfloat16
epsilon_mean = 1e-06


def dot(a, b):
    return jnp.dot(a, b, preferred_element_type=F32)


def loop(low, high, body):
    def step(index, carry):
        body(index)
        return carry

    lax.fori_loop(low, high, step, 0)


def aligned(index, size):
    return pl.ds(pl.multiple_of(index * size, size), size)


def kernel(
    dims,
    targets_ref,
    layers_ref,
    energies_ref,
    coulomb_ref,
    beta_prev_ref,
    current_hbm,
    previous_hbm,
    conduction_hbm,
    valence_hbm,
    exchange_hbm,
    screened_hbm,
    next_ref,
    alpha_ref,
    beta_ref,
    current,
    previous,
    conduction,
    valence,
    exchange,
    screened,
    outgoing,
    arrived,
    amps_t,
    gather_mat,
    slot_row,
    slot_col,
    layer_col,
    energy_col,
    part_v,
    part_e,
    pair_buf,
    chip_sum,
    reduced_in,
    low_send,
    proj_mine,
    proj_all,
    total_part,
    total_in,
    coupled_part,
    coupled_t,
    tile_out,
    coupled_all,
    direct_all,
    exchange_rows,
    kernel_out,
    returned,
    start,
    stats_mine,
    stats_in,
    stats_group,
    stats_all,
    hbm_sem,
    first_send,
    first_recv,
    pair_send,
    pair_recv,
    scatter_send,
    scatter_recv,
    half_send,
    half_recv,
    ring_send,
    ring_recv,
    gather_send,
    gather_recv,
    forward_send,
    forward_recv,
    last_send,
    last_recv,
    stat_send,
    stat_recv,
    stat_ring_send,
    stat_ring_recv,
):
    KR, B, NZ, CAP, OWN, SLOT, NG, NV = dims
    NB = B // 2
    NX = NB // NZ
    W = B // NZ
    GC = NG // NB
    GD = NG // B
    NH = NV // 2
    NK = NH // KR
    CH = SLOT // NZ
    LANE = min(128, NH)
    rows_total = OWN * KR * B

    g = lax.axis_index("kring")
    s = lax.axis_index("band")
    chip = s // 2
    core = lax.rem(s, 2)
    other = 1 - core
    plane = chip // NX
    column = lax.rem(chip, NX)
    partner = chip * 2 + other

    def chip_at(jc):
        return lax.rem(plane + jc // NX, NZ) * NX + lax.rem(column + lax.rem(jc, NX), NX)

    def chip_from(jc):
        return lax.rem(plane + NZ - jc // NX, NZ) * NX + lax.rem(column + NX - lax.rem(jc, NX), NX)

    def band_at(j):
        return chip_at(j // 2) * 2 + lax.rem(core + lax.rem(j, 2), 2)

    def band_from(j):
        return chip_from(j // 2) * 2 + lax.rem(core + lax.rem(j, 2), 2)

    def ring_at(k):
        return lax.rem(g + k, KR)

    def ring_from(k):
        return lax.rem(g + KR - k, KR)

    def remote(src, dst, send, recv, ring, band):
        return pltpu.make_async_remote_copy(
            src_ref=src,
            dst_ref=dst,
            send_sem=send,
            recv_sem=recv,
            device_id=(ring, band),
            device_id_type=MESH,
        )

    fetches = [
        pltpu.make_async_copy(src, dst, hbm_sem.at[i])
        for i, (src, dst) in enumerate(
            (
                (current_hbm, current),
                (valence_hbm, valence),
                (exchange_hbm, exchange),
                (previous_hbm, previous),
                (screened_hbm, screened),
                (conduction_hbm, conduction),
            )
        )
    ]
    for fetch in fetches:
        fetch.start()

    barrier = pltpu.get_barrier_semaphore()

    def greet_band(j):
        pl.semaphore_signal(barrier, inc=1, device_id=(g, band_at(j)), device_id_type=MESH)

    def greet_ring(k):
        pl.semaphore_signal(barrier, inc=1, device_id=(ring_at(k), s), device_id_type=MESH)

    loop(1, B, greet_band)
    loop(1, KR, greet_ring)

    blk = min(256, OWN)
    upper = (
        lax.broadcasted_iota(jnp.int32, (blk, blk), 0) <= lax.broadcasted_iota(jnp.int32, (blk, blk), 1)
    ).astype(F32).astype(BF16)
    carry = jnp.zeros((B, 1), F32)
    for b in range(OWN // blk):
        targets = targets_ref[:, b * blk : (b + 1) * blk]
        onehot = (lax.broadcasted_iota(jnp.int32, (B, blk), 0) == targets).astype(F32)
        counted = dot(onehot.astype(BF16), upper) + carry
        rank = jnp.sum(counted * onehot, axis=0, keepdims=True) - 1.0
        slot_row[:, b * blk : (b + 1) * blk] = targets.astype(F32) * CAP + rank
        carry = carry + jnp.sum(onehot, axis=1, keepdims=True)

    pl.semaphore_wait(barrier, B - 1 + KR - 1)
    fetches[0].wait()

    def first_copy(j):
        return remote(
            outgoing.at[j],
            arrived.at[pl.ds(pl.multiple_of(s * CAP, CAP), CAP), :],
            first_send.at[j],
            first_recv.at[j],
            g,
            band_at(j),
        )

    def place(target):
        wanted = (lax.broadcasted_iota(jnp.int32, (CAP, 1), 0) + target * CAP).astype(F32)
        pick = (wanted == slot_row[...]).astype(F32).astype(BF16)
        return dot(pick, current[...]).astype(BF16)

    def send_first(j):
        outgoing[j] = place(band_at(j))
        first_copy(j).start()

    loop(1, B, send_first)
    arrived[pl.ds(pl.multiple_of(s * CAP, CAP), CAP), :] = place(s)

    def column_of(row_ref, col_ref, count):
        def one(b):
            row = row_ref[:, aligned(b, LANE)].astype(F32)
            col_ref[aligned(b, LANE), :] = jnp.broadcast_to(row, (LANE, LANE)).T

        loop(0, count // LANE, one)

    column_of(slot_row, slot_col, OWN)
    column_of(layers_ref, layer_col, SLOT)
    column_of(energies_ref, energy_col, OWN)

    def build_gather(b):
        wanted = (lax.broadcasted_iota(jnp.int32, (1, LANE), 1) + b * LANE).astype(F32)
        gather_mat[:, aligned(b, LANE)] = (slot_col[...] == wanted).astype(F32).astype(BF16)

    loop(0, SLOT // LANE, build_gather)

    def wide(col, rows):
        return jnp.concatenate([col[rows, :]] * (NV // LANE), axis=1)

    tile = min(256, OWN)
    fetches[3].wait()

    def begin_start(b):
        rows = aligned(b, tile)
        start[rows, :] = wide(energy_col, rows) * current[rows, :].astype(F32) - beta_prev_ref[
            ...
        ] * previous[rows, :].astype(F32)

    loop(0, OWN // tile, begin_start)

    fetches[1].wait()
    fetches[2].wait()

    wide_tile = min(256, NG)

    def project(i):
        rows = aligned(lax.rem(plane + NZ - i, NZ), CH)
        amps = arrived[rows, :].astype(F32).T
        layers = layers_ref[:, rows]
        amps_t[i, 0:NV, :] = jnp.where(layers == 0, amps, 0.0).astype(BF16)
        amps_t[i, NV : 2 * NV, :] = jnp.where(layers == 1, amps, 0.0).astype(BF16)

    def accumulate(i, pairs, part):
        rows = aligned(lax.rem(plane + NZ - i, NZ), CH)

        def one(b):
            cols = aligned(b, wide_tile)
            more = dot(amps_t[i], pairs[rows, cols]).reshape(2, NV, wide_tile)
            if i == 0:
                part[:, :, cols] = more
            else:
                part[:, :, cols] += more

        loop(0, NG // wide_tile, one)

    for i in range(NZ):
        loop(max(1, i * W), (i + 1) * W, lambda j: first_copy(j).wait_recv())
        project(i)
        if i < NZ - 1:
            accumulate(i, valence, part_v)
            accumulate(i, exchange, part_e)

    def pair_copy(which, part):
        return remote(
            part.at[:, pl.ds(pl.multiple_of(other * NH, NH), NH), :],
            pair_buf.at[which],
            pair_send.at[which],
            pair_recv.at[which],
            g,
            partner,
        )

    def scatter_copy(which, jc):
        return remote(
            chip_sum.at[which, chip_at(jc)],
            reduced_in.at[which, jc],
            scatter_send.at[which, jc],
            scatter_recv.at[which, jc],
            g,
            chip_at(jc) * 2 + core,
        )

    def scatter(which, part):
        pair_copy(which, part).wait_recv()

        def one(jc):
            to = chip_at(jc)
            cols = aligned(to, GC)
            chip_sum[which, to] = (
                part[:, pl.ds(pl.multiple_of(core * NH, NH), NH), cols] + pair_buf[which, :, :, cols]
            ).astype(BF16)
            scatter_copy(which, jc).start()

        loop(1, NB, one)

    def reduce(which, part):
        cols = aligned(chip, GC)
        total = part[:, pl.ds(pl.multiple_of(core * NH, NH), NH), cols] + pair_buf[which, :, :, cols]
        for jc in range(1, NB):
            scatter_copy(which, jc).wait_recv()
            total = total + reduced_in[which, jc].astype(F32)
        return total

    accumulate(NZ - 1, valence, part_v)
    pair_copy(0, part_v).start()
    accumulate(NZ - 1, exchange, part_e)
    pair_copy(1, part_e).start()
    scatter(0, part_v)
    scatter(1, part_e)

    total = reduce(0, part_v)
    first_half = lax.broadcasted_iota(jnp.int32, (NH, GC), 1) < GD
    swapped = pltpu.roll(total[1], GD, 1)
    swapped_too = pltpu.roll(total[0], GD, 1)
    for_core = (
        jnp.where(first_half, total[0], swapped).astype(BF16),
        jnp.where(first_half, swapped_too, total[1]).astype(BF16),
    )
    mine = pl.ds(pl.multiple_of(core * NH, NH), NH)

    @pl.when(core == 0)
    def _():
        proj_mine[mine, :] = for_core[0]
        low_send[...] = for_core[1]

    @pl.when(core == 1)
    def _():
        proj_mine[mine, :] = for_core[1]
        low_send[...] = for_core[0]

    half_copy = remote(low_send, proj_mine.at[mine, :], half_send, half_recv, g, partner)
    half_copy.start()

    def ring_copy(k):
        return remote(
            proj_mine,
            proj_all.at[:, k * GC : (k + 1) * GC],
            ring_send.at[0, k],
            ring_recv.at[0, k],
            ring_at(k),
            s,
        )

    def total_copy(k):
        return remote(
            total_part.at[:, pl.ds(pl.multiple_of(ring_at(k) * NK, NK), NK), :],
            total_in.at[k],
            ring_send.at[1, k],
            ring_recv.at[1, k],
            ring_at(k),
            s,
        )

    def coupled_copy(k):
        return remote(
            coupled_part,
            coupled_t.at[:, pl.ds(pl.multiple_of(g * NK, NK), NK), :],
            ring_send.at[2, k],
            ring_recv.at[2, k],
            ring_at(k),
            s,
        )

    half_copy.wait_recv()
    for k in range(1, KR):
        ring_copy(k).start()
    proj_all[:, 0:GC] = proj_mine[...]

    total_part[...] = reduce(1, part_e)
    for k in range(1, KR):
        total_copy(k).start()

    fetches[4].wait()
    for k in range(1, KR):
        ring_copy(k).wait_recv()
    part_x = part_v
    pair_copy(0, part_v).wait_send()

    def direct_tile(b):
        cols = aligned(b, wide_tile)
        for layer in range(2):
            part_x[layer, :, cols] = dot(proj_all[...], screened[layer, :, cols])

    loop(0, NG // wide_tile, direct_tile)
    pair_copy(2, part_x).start()

    ring_total = total_part[:, pl.ds(pl.multiple_of(g * NK, NK), NK), :]
    for k in range(1, KR):
        total_copy(k).wait_recv()
        ring_total = ring_total + total_in[k]
    here = aligned(chip, GC)
    coupled_part[0] = coulomb_ref[0:1, here] * ring_total[0] + coulomb_ref[1:2, here] * ring_total[1]
    coupled_part[1] = coulomb_ref[2:3, here] * ring_total[0] + coulomb_ref[3:4, here] * ring_total[1]
    for k in range(1, KR):
        coupled_copy(k).start()
    coupled_t[:, pl.ds(pl.multiple_of(g * NK, NK), NK), :] = coupled_part[...]

    scatter(2, part_x)

    half_cols = pl.ds(pl.multiple_of(core * NH, NH), NH)

    def gather_copy(which, full, jc):
        return remote(
            tile_out.at[which],
            full.at[:, aligned(chip, GC), half_cols],
            gather_send.at[which, jc],
            gather_recv.at[which, jc],
            g,
            chip_at(jc) * 2 + core,
        )

    def forward_copy(which, full, jc):
        block = full.at[:, aligned(chip_from(jc), GC), half_cols]
        return remote(
            block, block, forward_send.at[which, jc], forward_recv.at[which, jc], g, partner
        )

    def spread(which, full, block_t):
        for layer in range(2):
            tile_out[which, layer] = block_t[layer].T.astype(BF16)
        loop(1, NB, lambda jc: gather_copy(which, full, jc).start())
        full[:, aligned(chip, GC), half_cols] = tile_out[which]
        forward_copy(which, full, 0).start()

    def collect(which, full):
        def one(jc):
            gather_copy(which, full, jc).wait_recv()
            forward_copy(which, full, jc).start()

        loop(1, NB, one)

    for k in range(1, KR):
        coupled_copy(k).wait_recv()
    spread(0, coupled_all, coupled_t[...])
    direct_block = reduce(2, part_x)
    spread(1, direct_all, direct_block)
    collect(0, coupled_all)
    loop(0, NB, lambda jc: forward_copy(0, coupled_all, jc).wait_recv())

    pair_rows = 2 * CAP

    def exchange_tile(b):
        rows = aligned(b, pair_rows)
        zero = dot(exchange[rows, :], coupled_all[0])
        one = dot(exchange[rows, :], coupled_all[1])
        exchange_rows[rows, :] = 2.0 * jnp.where(wide(layer_col, rows) == 0.0, zero, one)

    loop(0, NB, exchange_tile)
    fetches[5].wait()
    collect(1, direct_all)
    loop(0, NB, lambda jc: forward_copy(1, direct_all, jc).wait_recv())

    def last_copy(j):
        to = band_at(j)
        return remote(
            kernel_out.at[pl.ds(pl.multiple_of(to * CAP, CAP), CAP), :],
            returned.at[pl.ds(pl.multiple_of(s * CAP, CAP), CAP), :],
            last_send.at[j],
            last_recv.at[j],
            g,
            to,
        )

    def kernel_tile(jc):
        rows = aligned(chip_at(jc), pair_rows)
        zero = dot(conduction[rows, :], direct_all[0])
        one = dot(conduction[rows, :], direct_all[1])
        direct = jnp.where(wide(layer_col, rows) == 0.0, zero, one)
        kernel_out[rows, :] = (exchange_rows[rows, :] - direct).astype(BF16)

    def kernel_step(jc):
        kernel_tile(jc)
        last_copy(2 * jc).start()
        last_copy(2 * jc + 1).start()

    loop(1, NB, kernel_step)
    kernel_tile(0)
    last_copy(1).start()
    own = pl.ds(pl.multiple_of(s * CAP, CAP), CAP)
    returned[own, :] = kernel_out[own, :]

    for i in range(NZ):
        loop(max(1, i * W), (i + 1) * W, lambda j: last_copy(j).wait_recv())
        slots = aligned(lax.rem(plane + NZ - i, NZ), CH)

        def add_rows(b, slots=slots):
            rows = aligned(b, tile)
            start[rows, :] += dot(gather_mat[rows, slots], returned[slots, :])

        loop(0, OWN // tile, add_rows)

    def fold(b, sums):
        rows = aligned(b, tile)
        cur = current[rows, :].astype(F32)
        return (
            sums[0] + jnp.sum(cur * start[rows, :], axis=0, keepdims=True),
            sums[1] + jnp.sum(cur * cur, axis=0, keepdims=True),
        )

    none = jnp.zeros((1, NV), F32)
    cross, square = lax.fori_loop(0, OWN // tile, fold, (none, none))

    def ratio(above, below):
        return above / jnp.where(below == 0.0, 1.0, below)

    local = ratio(cross, square)

    def fold_rest(b, acc):
        rows = aligned(b, tile)
        rest = start[rows, :] - local * current[rows, :].astype(F32)
        return acc + jnp.sum(rest * rest, axis=0, keepdims=True)

    rest_sq = lax.fori_loop(0, OWN // tile, fold_rest, none)

    def combine(read, count):
        cross = sum(read(i)[0:1] for i in range(count))
        square = sum(read(i)[1:2] for i in range(count))
        alpha = ratio(cross, square)
        rest = none
        for i in range(count):
            item = read(i)
            apart = ratio(item[0:1], item[1:2]) - alpha
            rest = rest + (item[2:3] + apart * apart * item[1:2])
        return cross, square, rest

    stats_mine[...] = jnp.concatenate([cross, square, rest_sq] + [none] * 5, axis=0)

    def stat_copy(j):
        return remote(stats_mine, stats_in.at[s], stat_send.at[j], stat_recv.at[j], g, band_at(j))

    def stat_ring_copy(k):
        return remote(
            stats_group, stats_all.at[g], stat_ring_send.at[k], stat_ring_recv.at[k], ring_at(k), s
        )

    loop(1, B, lambda j: stat_copy(j).start())
    stats_in[s] = stats_mine[...]
    loop(1, B, lambda j: stat_copy(j).wait_recv())
    stats_group[...] = jnp.concatenate(
        list(combine(lambda i: stats_in[i], B)) + [none] * 5, axis=0
    )
    loop(1, KR, lambda k: stat_ring_copy(k).start())
    stats_all[g] = stats_group[...]
    loop(1, KR, lambda k: stat_ring_copy(k).wait_recv())
    cross, square, rest_sq = combine(lambda i: stats_all[i], KR)

    alpha = cross / square
    beta = jnp.sqrt(rest_sq / rows_total + epsilon_mean)
    alpha_ref[...] = alpha
    beta_ref[...] = beta

    def finish(b):
        rows = aligned(b, tile)
        next_ref[rows, :] = (
            (start[rows, :] - alpha * current[rows, :].astype(F32)) / beta
        ).astype(BF16)

    loop(0, OWN // tile, finish)

    loop(1, B, lambda j: first_copy(j).wait_send())
    pair_copy(1, part_e).wait_send()
    pair_copy(2, part_x).wait_send()
    half_copy.wait_send()
    for which in range(3):
        loop(1, NB, lambda jc, which=which: scatter_copy(which, jc).wait_send())
    for k in range(1, KR):
        ring_copy(k).wait_send()
        total_copy(k).wait_send()
        coupled_copy(k).wait_send()
    for which, full in ((0, coupled_all), (1, direct_all)):
        loop(1, NB, lambda jc, which=which, full=full: gather_copy(which, full, jc).wait_send())
        loop(0, NB, lambda jc, which=which, full=full: forward_copy(which, full, jc).wait_send())
    loop(1, B, lambda j: last_copy(j).wait_send())
    loop(1, B, lambda j: stat_copy(j).wait_send())
    loop(1, KR, lambda k: stat_ring_copy(k).wait_send())


def per_device(
    planes,
    current,
    previous,
    energies,
    targets,
    layer_ids,
    conduction_pairs,
    valence_pairs,
    exchange_pairs,
    screened,
    coulomb,
    beta_prev,
):
    KR, B = lax.axis_size("kring"), lax.axis_size("band")
    OWN, NV = current.shape
    SLOT, NG = conduction_pairs.shape
    CAP = SLOT // B
    NB = B // 2
    NH = NV // 2
    GC = NG // NB
    GD = NG // B
    NK = NH // KR
    CH = SLOT // planes
    LANE = min(128, NH)
    by_layer = jnp.transpose(screened, (3, 0, 1, 2, 4)).reshape(2, KR * 2 * GD, NG)
    vmem = pltpu.VMEM
    dma = pltpu.SemaphoreType.DMA
    scratch = [
        vmem((OWN, NV), BF16),
        vmem((OWN, NV), BF16),
        vmem((SLOT, NG), BF16),
        vmem((SLOT, NG), BF16),
        vmem((SLOT, NG), BF16),
        vmem((2, KR * 2 * GD, NG), BF16),
        vmem((B, CAP, NV), BF16),
        vmem((SLOT, NV), BF16),
        vmem((planes, 2 * NV, CH), BF16),
        vmem((OWN, SLOT), BF16),
        vmem((1, OWN), F32),
        vmem((OWN, LANE), F32),
        vmem((SLOT, LANE), F32),
        vmem((OWN, LANE), F32),
        vmem((2, NV, NG), F32),
        vmem((2, NV, NG), F32),
        vmem((3, 2, NH, NG), F32),
        vmem((3, NB, 2, NH, GC), BF16),
        vmem((3, NB, 2, NH, GC), BF16),
        vmem((NH, GC), BF16),
        vmem((NV, GC), BF16),
        vmem((NV, KR * GC), BF16),
        vmem((2, NH, GC), F32),
        vmem((KR, 2, NK, GC), F32),
        vmem((2, NK, GC), F32),
        vmem((2, NH, GC), F32),
        vmem((2, 2, GC, NH), BF16),
        vmem((2, NG, NV), BF16),
        vmem((2, NG, NV), BF16),
        vmem((SLOT, NV), F32),
        vmem((SLOT, NV), BF16),
        vmem((SLOT, NV), BF16),
        vmem((OWN, NV), F32),
        vmem((8, NV), F32),
        vmem((B, 8, NV), F32),
        vmem((8, NV), F32),
        vmem((KR, 8, NV), F32),
        dma((6,)),
        dma((B,)),
        dma((B,)),
        dma((3,)),
        dma((3,)),
        dma((3, NB)),
        dma((3, NB)),
        dma,
        dma,
        dma((3, KR)),
        dma((3, KR)),
        dma((2, NB)),
        dma((2, NB)),
        dma((2, NB)),
        dma((2, NB)),
        dma((B,)),
        dma((B,)),
        dma((B,)),
        dma((B,)),
        dma((KR,)),
        dma((KR,)),
    ]
    in_vmem = pl.BlockSpec(memory_space=pltpu.VMEM)
    in_hbm = pl.BlockSpec(memory_space=pl.ANY)
    next_vector, alpha, beta = pl.pallas_call(
        functools.partial(kernel, (KR, B, planes, CAP, OWN, SLOT, NG, NV)),
        out_shape=(
            jax.ShapeDtypeStruct((OWN, NV), BF16),
            jax.ShapeDtypeStruct((1, NV), F32),
            jax.ShapeDtypeStruct((1, NV), F32),
        ),
        in_specs=[in_vmem] * 5 + [in_hbm] * 6,
        out_specs=(in_vmem, in_vmem, in_vmem),
        scratch_shapes=scratch,
        compiler_params=pltpu.CompilerParams(
            collective_id=0, has_side_effects=True, vmem_limit_bytes=62 * 1024 * 1024
        ),
    )(
        targets.reshape(1, OWN),
        layer_ids.reshape(1, SLOT),
        energies.reshape(1, OWN),
        coulomb.reshape(4, NG),
        beta_prev.reshape(1, NV),
        current,
        previous,
        conduction_pairs,
        valence_pairs,
        exchange_pairs,
        by_layer,
    )
    return next_vector, alpha.reshape(NV), beta.reshape(NV)


def solution(mesh):
    in_specs = (
        P(("kring", "band"), None),
        P(("kring", "band"), None),
        P(("kring", "band")),
        P(("kring", "band")),
        P(("kring", "band")),
        P(("kring", "band"), None),
        P(("kring", "band"), None),
        P(("kring", "band"), None),
        P(None, None, "band", None, None),
        P(),
        P(),
    )
    out_specs = (P(("kring", "band"), None), P(), P())
    planes = max(2, mesh.shape["band"] // 4)
    return jax.shard_map(
        functools.partial(per_device, planes),
        mesh=mesh,
        in_specs=in_specs,
        out_specs=out_specs,
        check_vma=False,
    )
```

time: 530 us -> 133 us (0.25)
  blocking collectives: 353 us -> 0 us
  Pallas kernels: 0 us -> 120 us
  waiting for transfers between devices: 64.9 us -> 0 us
  matrix products: 29.5 us -> 0 us
  local copies, waits for them, and re-layouts: 38.2 us -> 12.9 us
  other arithmetic: 19.5 us -> 0 us
  between operations: 14.9 us -> 0.64 us
  starting transfers between devices: 9.51 us -> 0 us
    psum x3 -> x0, blocking collectives: 218 us -> none  [the longest x1 91.2 us: per_device(): direct = lax.psum(direct_part, 'band').astype(jnp.bfloat16)]
    pallas_call x0 -> x1, Pallas kernels: none -> 120 us  [per_device(): pl.pallas_call(functools.partial(kernel, (KR, B, planes, CAP, OWN, SLOT,...]
    unnamed x1 -> x0, blocking collectives: 84.6 us -> none
    psum x1 -> x0, waiting for transfers between devices: 64.9 us -> none  [per_device(): exchange_total = lax.psum(exchange_part, ('kring', 'band'))]
    dot_general x5 -> x0, matrix products: 29.5 us -> none  [the longest x1 7.32 us: per_device(): jnp.einsum('tg,lgn->tln', conduction_pairs, direct, preferred_element_typ...]
    all_to_all x1 -> x0, blocking collectives: 25.4 us -> none  [per_device(): lax.all_to_all(kernel_rows.reshape(band_count, capacity, chains), 'band',...]
    all_gather x1 -> x0, blocking collectives: 25.1 us -> none  [per_device(): pieces = lax.all_gather(projected[None], 'kring', axis=0, tiled=True)]
    gather x2 -> x0, local copies, waits for them, and re-layouts: 19.5 us -> none  [the longest x1 12 us: per_device(): blocks = jnp.take(screened, distance, axis=0)]
  transfers between devices with their start and end apart: 2 -> 0, of which waited for: 1 -> 0; matrix products, arithmetic and copies ran while one was open for 5% -> 0% of each run, Pallas kernels for 0% -> 0%
where the time goes in v1:
time: 133 us
  Pallas kernels  120 us (90%)
  local copies, waits for them, and re-layouts  12.9 us (10%)
    pallas_call x1, Pallas kernels, per_device(): pl.pallas_call(functools.partial(kernel, (KR, B, planes, CAP, OWN, SLOT,...  120 us
    transpose x1, local copies, waits for them, and re-layouts, per_device(): jnp.transpose(screened, (3, 0, 1, 2, 4)).reshape(2, KR * 2 * GD, NG)  5.48 us
    unnamed x3, local copies, waits for them, and re-layouts  4.74 us

profile of v1, /device:TPU:1, one launch (start us, length us, event | category | flops | bytes accessed | tf_op | source)
XLA Modules:
  0.0 133.1 jit_solution(8283169181905282337)
XLA Ops:
  0.6 1.3 reshape.31.layers_ref
  1.9 1.3 %reshape.33.coulomb_ref = f32[4,1024]{1,0:T(4,128)} reshape(f32[2,2,1024]{2,1,0:T(2,128)} %param.20) | data formatting | bytes 32768 | tf_op jit(solution)/shard_map/reshape | solution.py:706
  3.3 5.5 %copy.14 = bf16[2,8,2,64,1024]{4,3,2,1,0:T(8,128)(2,1)} copy(bf16[2,8,2,64,1024]{4,0,3,2,1:T(2,128)(2,1)} %bitcast.8) | data formatting | bytes 8388608 | tf_op jit(solution)/shard_map/transpose | solution.py:624
  8.8 119.6 %shard_map.130 = (bf16[2048,256]{1,0:T(8,128)(2,1)}, f32[1,256]{1,0:T(1,128)}, f32[1,256]{1,0:T(1,128)}) custom-call(s32[1,2048]{1,0:T(1,128)} %bitcast.9, s32[1,2560]{1,0:T(1,128)} %reshape.31.layers_ref, f32[1,2048]{1,0:T(1,128)} %bitcast.10, f32[4,1024]{1,0:T(4,128)} %reshape.33.coulomb_ref, f32[1,256]{1,0:T(1,128)} %bitcast.11, ...), custom_call_target="tpu_custom_call" | custom-call | tf_op jit(solution)/shard_map/pallas_call | solution.py:689
  128.3 2.3 %copy.18 = bf16[2048,256]{1,0:T(8,128)(2,1)} copy(bf16[2048,256]{1,0:T(8,128)(2,1)} %get-tuple-element.12) | data formatting | bytes 2097152
  130.6 1.2 copy.19
  131.8 1.2 copy.20

commit v2 on v1

v2 whole, which is shorter than its diff:
```python
import functools

import jax
import jax.numpy as jnp
from jax import lax
from jax.experimental import pallas as pl
from jax.experimental.pallas import tpu as pltpu
from jax.sharding import PartitionSpec as P

MESH = pl.DeviceIdType.MESH
F32 = jnp.float32
BF16 = jnp.bfloat16
epsilon_mean = 1e-06


def dot(a, b):
    return jnp.dot(a, b, preferred_element_type=F32)


def loop(low, high, body):
    def step(index, carry):
        body(index)
        return carry

    lax.fori_loop(low, high, step, 0)


def aligned(index, size):
    return pl.ds(pl.multiple_of(index * size, size), size)


def kernel(
    dims,
    targets_ref,
    layers_ref,
    energies_ref,
    coulomb_ref,
    beta_prev_ref,
    current_hbm,
    previous_hbm,
    conduction_hbm,
    valence_hbm,
    exchange_hbm,
    raw_hbm,
    start,
    lanczos,
    current,
    previous,
    valence,
    exchange,
    raw,
    screened,
    outgoing,
    arrived,
    amps_t,
    gather_mat,
    slot_row,
    layer_row,
    slot_col,
    layer_col,
    energy_col,
    part_v,
    part_e,
    pair_buf,
    chip_sum,
    reduced_in,
    chip_sum_e,
    reduced_e,
    proj_mine,
    proj_all,
    part_x,
    total_part,
    total_in,
    coupled_part,
    coupled_t,
    coupled_tile,
    direct_tile,
    coupled_all,
    direct_all,
    exchange_rows,
    kernel_out,
    returned,
    stats_mine,
    stats_in,
    stats_group,
    stats_all,
    hbm_sem,
    raw_sem,
    first_send,
    first_recv,
    pair_send,
    pair_recv,
    scatter_send,
    scatter_recv,
    share_send,
    share_recv,
    ring_send,
    ring_recv,
    y_send,
    y_recv,
    layer_send,
    layer_recv,
    coupled_send,
    coupled_recv,
    gather_send,
    gather_recv,
    forward_send,
    forward_recv,
    last_send,
    last_recv,
    stat_send,
    stat_recv,
    stat_ring_send,
    stat_ring_recv,
):
    KR, B, NZ, CAP, OWN, SLOT, NG, NV = dims
    NB = B // 2
    NX = NB // NZ
    W = B // NZ
    GC = NG // NB
    GD = NG // B
    NH = NV // 2
    CH = SLOT // NZ
    LANE = min(128, NH)
    rows_total = OWN * KR * B
    conduction = valence

    g = lax.axis_index("kring")
    s = lax.axis_index("band")
    chip = s // 2
    core = lax.rem(s, 2)
    other = 1 - core
    plane = chip // NX
    column = lax.rem(chip, NX)
    partner = chip * 2 + other

    planes_at = [lax.rem(plane + i, NZ) for i in range(NZ)]
    columns_at = [lax.rem(column + i, NX) for i in range(NX)]
    rings_at = [lax.rem(g + k, KR) for k in range(KR)]
    cores_at = (core, other)
    chips_at = [planes_at[jc // NX] * NX + columns_at[jc % NX] for jc in range(NB)]
    chips_from = [planes_at[-(jc // NX) % NZ] * NX + columns_at[-(jc % NX) % NX] for jc in range(NB)]
    peers_at = [chips_at[j // 2] * 2 + cores_at[j % 2] for j in range(B)]

    phases = (
        sorted({1, NZ - 1}),
        [i for i in range(NZ) if i not in (1, NZ - 1)][::-1],
    )
    plane_order = phases[0] + phases[1]
    away = [i * NX + t for i in plane_order for t in reversed(range(NX)) if i + t > 0]

    def chips_of(planes):
        return [i * NX + t for i in planes for t in reversed(range(NX))]

    def peers_of(planes):
        return [2 * jc + t for jc in chips_of(planes) for t in (1, 0) if jc + t > 0]

    KY = KR // 2
    GY = NG // KY
    NQ = 2 * NB
    NE = NH // NQ
    ring_y = g // 2
    ring_x = lax.rem(g, 2)
    ys_at = [lax.rem(ring_y + t, KY) for t in range(KY)]
    xs_at = (ring_x, 1 - ring_x)
    layer_at = [(xs_at[q // NB], chips_at[q % NB]) for q in range(NQ)]
    layer_here = ring_x * NB + chip

    def remote(src, dst, send, recv, ring, band):
        return pltpu.make_async_remote_copy(
            src_ref=src,
            dst_ref=dst,
            send_sem=send,
            recv_sem=recv,
            device_id=(ring, band),
            device_id_type=MESH,
        )

    waits = []
    later = waits.append

    def drain():
        for wait in waits:
            wait()

    fetches = [
        pltpu.make_async_copy(src, dst, hbm_sem.at[i])
        for i, (src, dst) in enumerate(
            (
                (current_hbm, current),
                (valence_hbm, valence),
                (exchange_hbm, exchange),
                (previous_hbm, previous),
                (conduction_hbm, conduction),
            )
        )
    ]
    fetches[0].start()

    barrier = pltpu.get_barrier_semaphore()
    for j in range(1, B):
        pl.semaphore_signal(barrier, inc=1, device_id=(g, peers_at[j]), device_id_type=MESH)
    for k in range(1, KR):
        pl.semaphore_signal(barrier, inc=1, device_id=(rings_at[k], s), device_id_type=MESH)
    for x, c in layer_at[NB + 1 :]:
        pl.semaphore_signal(
            barrier, inc=1, device_id=(ring_y * 2 + x, c * 2 + core), device_id_type=MESH
        )

    blk = min(256, OWN)
    upper = (
        lax.broadcasted_iota(jnp.int32, (blk, blk), 0) <= lax.broadcasted_iota(jnp.int32, (blk, blk), 1)
    ).astype(F32).astype(BF16)
    carry = jnp.zeros((B, 1), F32)
    for b in range(OWN // blk):
        targets = targets_ref[:, b * blk : (b + 1) * blk]
        onehot = (lax.broadcasted_iota(jnp.int32, (B, blk), 0) == targets).astype(F32)
        counted = dot(onehot.astype(BF16), upper) + carry
        rank = jnp.sum(counted * onehot, axis=0, keepdims=True) - 1.0
        slot_row[:, b * blk : (b + 1) * blk] = targets.astype(F32) * CAP + rank
        carry = carry + jnp.sum(onehot, axis=1, keepdims=True)

    fetches[0].wait()

    def raw_fetch(ka):
        slot = lax.rem(ka, 2)
        return pltpu.make_async_copy(raw_hbm.at[ka], raw.at[slot], raw_sem.at[slot])

    raw_fetch(0).start()
    for fetch in fetches[1:4]:
        fetch.start()

    def first_copy(j):
        return remote(
            outgoing.at[j],
            arrived.at[aligned(s, CAP), :],
            first_send.at[j],
            first_recv.at[j],
            g,
            peers_at[j],
        )

    def place(target):
        wanted = (lax.broadcasted_iota(jnp.int32, (CAP, 1), 0) + target * CAP).astype(F32)
        pick = (wanted == slot_row[...]).astype(F32).astype(BF16)
        return dot(pick, current[...]).astype(BF16)

    for j in range(1, B):
        outgoing[j] = place(peers_at[j])
    arrived[aligned(s, CAP), :] = place(s)
    pl.semaphore_wait(barrier, B - 1 + KR - 1 + NB - 1)
    for j in peers_of(phases[0]):
        first_copy(j).start()

    def column_of(row_ref, col_ref, count):
        def one(b):
            row = row_ref[:, aligned(b, LANE)].astype(F32)
            col_ref[aligned(b, LANE), :] = jnp.broadcast_to(row, (LANE, LANE)).T

        loop(0, count // LANE, one)

    for b in range(SLOT // LANE):
        row = layers_ref[b : b + 1, :].astype(F32)
        layer_row[:, b * LANE : (b + 1) * LANE] = row
        layer_col[b * LANE : (b + 1) * LANE, :] = jnp.broadcast_to(row, (LANE, LANE)).T
    GL = min(128, NG)
    JH = 2 * (NG // GL)
    PB = min(GD, 256 // JH)
    place_to = lax.broadcasted_iota(jnp.int32, (JH * PB, JH * PB), 0)
    place_from = lax.broadcasted_iota(jnp.int32, (JH * PB, JH * PB), 1)
    part_layers = (
        (place_to - (place_to // PB) * PB) * JH + place_to // PB == place_from
    ).astype(F32).astype(BF16)

    def part(ka):
        raw_fetch(ka).wait()

        @pl.when(ka + 1 < 2 * KR)
        def _():
            raw_fetch(ka + 1).start()

        slot = lax.rem(ka, 2)
        for b in range(GD // PB):
            rows = dot(part_layers, raw[slot, b * PB * JH : (b + 1) * PB * JH, :]).astype(BF16)
            for jh in range(JH):
                screened[jh % 2, ka, core, b * PB : (b + 1) * PB, jh // 2 * GL : (jh // 2 + 1) * GL] = (
                    rows[jh * PB : (jh + 1) * PB]
                )

    loop(0, 2 * KR, part)
    for j in peers_of(phases[0]):
        first_copy(j).wait_send()
    for j in peers_of(phases[1]):
        first_copy(j).start()
        later(first_copy(j).wait_send)
    shared = screened.at[:, :, core]
    share = remote(shared, shared, share_send, share_recv, g, partner)
    share.start()
    later(share.wait_send)

    def build_gather():
        column_of(slot_row, slot_col, OWN)

        def one(b):
            wanted = (lax.broadcasted_iota(jnp.int32, (1, LANE), 1) + b * LANE).astype(F32)
            gather_mat[:, aligned(b, LANE)] = (slot_col[...] == wanted).astype(F32).astype(BF16)

        loop(0, SLOT // LANE, one)

    def wide(col, rows):
        return jnp.concatenate([col[rows, :]] * (NV // LANE), axis=1)

    tile = min(256, OWN)

    def build_start():
        column_of(energies_ref, energy_col, OWN)

        def one(b):
            rows = aligned(b, tile)
            start[rows, :] = wide(energy_col, rows) * current[rows, :].astype(F32) - beta_prev_ref[
                ...
            ] * previous[rows, :].astype(F32)

        loop(0, OWN // tile, one)

    for fetch in fetches[1:4]:
        fetch.wait()

    plane_cols = NX * GC

    def source_rows(i):
        return aligned(planes_at[-i % NZ], CH)

    def project(i):
        amps = arrived[source_rows(i), :].astype(F32).T
        layers = layer_row[:, source_rows(i)]
        amps_t[i, 0:NV, :] = jnp.where(layers == 0.0, amps, 0.0).astype(BF16)
        amps_t[i, NV : 2 * NV, :] = jnp.where(layers == 1.0, amps, 0.0).astype(BF16)

    def accumulate(phase, pairs, part, cols):
        more = sum(dot(amps_t[i], pairs[source_rows(i), cols]) for i in phases[phase])
        more = more.reshape(2, NV, plane_cols)
        if phase == 0:
            part[:, :, cols] = more
        else:
            part[:, :, cols] += more

    for phase in range(2):
        for j in peers_of(phases[phase]):
            first_copy(j).wait_recv()
        for i in phases[phase]:
            project(i)
        if phase == 0:
            for pairs, part in ((valence, part_v), (exchange, part_e)):
                loop(
                    0,
                    NZ,
                    lambda b, pairs=pairs, part=part: accumulate(
                        0, pairs, part, aligned(b, plane_cols)
                    ),
                )

    mine = aligned(core, NH)
    here = aligned(chip, GC)

    def pair_copy(which, part, i):
        cols = aligned(planes_at[i], plane_cols)
        return remote(
            part.at[:, aligned(other, NH), cols],
            pair_buf.at[which, :, :, cols],
            pair_send.at[which, i],
            pair_recv.at[which, i],
            g,
            partner,
        )

    def pair_sum(which, part, i):
        cols = aligned(planes_at[i], plane_cols)
        accumulate(1, (valence, exchange)[which], part, cols)
        pair_copy(which, part, i).start()
        later(pair_copy(which, part, i).wait_send)

    def scatter_copy(which, jc):
        return remote(
            chip_sum.at[which, jc],
            reduced_in.at[which, jc],
            scatter_send.at[which, jc],
            scatter_recv.at[which, jc],
            g,
            chips_at[jc] * 2 + core,
        )

    def chip_part(which, part, jc):
        cols = aligned(chips_at[jc], GC)
        return part[:, mine, cols] + pair_buf[which, :, :, cols]

    def direct_part(which, part, jc):
        return part[:, :, aligned(chips_at[jc], GC)]

    def send_part(which, jc, value):
        chip_sum[which, jc] = value.astype(BF16)
        scatter_copy(which, jc).start()
        later(scatter_copy(which, jc).wait_send)

    def scatter(which, part):
        for i in plane_order:
            pair_copy(which, part, i).wait_recv()
            for jc in range((i + 1) * NX - 1, max(i * NX - 1, 0), -1):
                send_part(which, jc, chip_part(which, part, jc))

    def reduce(which, part, read):
        total = read(which, part, 0)
        for jc in away:
            scatter_copy(which, jc).wait_recv()
            total = total + reduced_in[which, jc].astype(F32)
        return total

    for i in plane_order:
        pair_sum(0, part_v, i)
    for i in plane_order:
        pair_sum(1, part_e, i)
    scatter(0, part_v)

    def over_y(t):
        return remote(
            chip_sum_e.at[t],
            reduced_e.at[t],
            y_send.at[0, t],
            y_recv.at[0, t],
            ys_at[t] * 2 + ring_x,
            s,
        )

    def exchange_part(t):
        cols = aligned(ys_at[t], GY)
        return part_e[:, mine, cols] + pair_buf[1, :, :, cols]

    for i in plane_order:
        pair_copy(1, part_e, i).wait_recv()
    y_order = sorted(range(1, KY), key=lambda t: -min(t, KY - t))
    for t in y_order:
        chip_sum_e[t] = exchange_part(t).astype(BF16)
        over_y(t).start()
        later(over_y(t).wait_send)

    total = reduce(0, part_v, chip_part)
    for layer in range(2):
        proj_mine[:, layer * GC : (layer + 1) * GC] = total[layer].astype(BF16)

    def ring_copy(k):
        return remote(
            proj_mine,
            proj_all.at[:, 2 * k * GC : 2 * (k + 1) * GC],
            ring_send.at[k],
            ring_recv.at[k],
            rings_at[k],
            s,
        )

    for k in range(1, KR):
        ring_copy(k).start()
        later(ring_copy(k).wait_send)
    proj_all[:, 0 : 2 * GC] = proj_mine[...]

    total_e = exchange_part(0)
    for t in y_order:
        over_y(t).wait_recv()
        total_e = total_e + reduced_e[t].astype(F32)
    total_part[...] = total_e

    def over_layer(q):
        x, c = layer_at[q]
        return remote(
            total_part.at[:, aligned(x * NB + c, NE), :],
            total_in.at[q],
            layer_send.at[0, q],
            layer_recv.at[0, q],
            ring_y * 2 + x,
            c * 2 + core,
        )

    def coupled_copy(q):
        x, c = layer_at[q]
        return remote(
            coupled_part,
            coupled_t.at[:, aligned(layer_here, NE), :],
            layer_send.at[1, q],
            layer_recv.at[1, q],
            ring_y * 2 + x,
            c * 2 + core,
        )

    for q in range(1, NQ):
        over_layer(q).start()
        later(over_layer(q).wait_send)
    build_gather()
    layer_total = total_part[:, aligned(layer_here, NE), :]
    for q in range(1, NQ):
        over_layer(q).wait_recv()
        layer_total = layer_total + total_in[q]
    quarter = aligned(ring_y, GY)
    for layer in range(2):
        coupled_part[layer] = (
            coulomb_ref[layer, 0:1, quarter] * layer_total[0]
            + coulomb_ref[layer, 1:2, quarter] * layer_total[1]
        )
    for q in range(1, NQ):
        coupled_copy(q).start()
        later(coupled_copy(q).wait_send)
    coupled_t[:, aligned(layer_here, NE), :] = coupled_part[...]

    fetches[4].start()
    share.wait_recv()
    for k in range(1, KR):
        ring_copy(k).wait_recv()
    for i in plane_order:
        cols = aligned(planes_at[i], plane_cols)
        for layer in range(2):
            part_x[layer, :, cols] = dot(
                proj_all[...], screened[layer, :, :, :, cols].reshape(2 * KR * GC, plane_cols)
            )
        for jc in range((i + 1) * NX - 1, max(i * NX - 1, 0), -1):
            send_part(1, jc, direct_part(1, part_x, jc))

    def y_copy(t):
        return remote(
            coupled_tile,
            coupled_all.at[:, quarter, mine],
            y_send.at[1, t],
            y_recv.at[1, t],
            ys_at[t] * 2 + ring_x,
            s,
        )

    def coupled_forward(t):
        block = coupled_all.at[:, aligned(ys_at[-t % KY], GY), mine]
        return remote(
            block, block, coupled_send.at[t], coupled_recv.at[t], g, partner
        )

    for q in range(1, NQ):
        coupled_copy(q).wait_recv()
    for layer in range(2):
        coupled_tile[layer] = coupled_t[layer].T.astype(BF16)
    for t in y_order:
        y_copy(t).start()
        later(y_copy(t).wait_send)
    coupled_all[:, quarter, mine] = coupled_tile[...]
    coupled_forward(0).start()
    later(coupled_forward(0).wait_send)
    build_start()

    def gather_copy(jc):
        return remote(
            direct_tile,
            direct_all.at[:, here, mine],
            gather_send.at[jc],
            gather_recv.at[jc],
            g,
            chips_at[jc] * 2 + core,
        )

    def forward_copy(jc):
        block = direct_all.at[:, aligned(chips_from[jc], GC), mine]
        return remote(block, block, forward_send.at[jc], forward_recv.at[jc], g, partner)

    direct_block = reduce(1, part_x, direct_part)
    for layer in range(2):
        direct_tile[layer] = direct_block[layer].T.astype(BF16)
    for jc in away:
        gather_copy(jc).start()
        later(gather_copy(jc).wait_send)
    direct_all[:, here, mine] = direct_tile[...]
    forward_copy(0).start()
    later(forward_copy(0).wait_send)
    for t in y_order:
        y_copy(t).wait_recv()
        coupled_forward(t).start()
        later(coupled_forward(t).wait_send)
    for t in range(KY):
        coupled_forward(t).wait_recv()

    pair_rows = 2 * CAP

    def exchange_tile(b):
        rows = aligned(b, pair_rows)
        zero = dot(exchange[rows, :], coupled_all[0])
        one = dot(exchange[rows, :], coupled_all[1])
        exchange_rows[rows, :] = 2.0 * jnp.where(wide(layer_col, rows) == 0.0, zero, one)

    loop(0, NB, exchange_tile)
    fetches[4].wait()
    for jc in away:
        gather_copy(jc).wait_recv()
        forward_copy(jc).start()
        later(forward_copy(jc).wait_send)
    for jc in range(NB):
        forward_copy(jc).wait_recv()

    def last_copy(j):
        return remote(
            kernel_out.at[aligned(peers_at[j], CAP), :],
            returned.at[aligned(s, CAP), :],
            last_send.at[j],
            last_recv.at[j],
            g,
            peers_at[j],
        )

    def kernel_tile(jc):
        rows = aligned(chips_at[jc], pair_rows)
        zero = dot(conduction[rows, :], direct_all[0])
        one = dot(conduction[rows, :], direct_all[1])
        direct = jnp.where(wide(layer_col, rows) == 0.0, zero, one)
        kernel_out[rows, :] = (exchange_rows[rows, :] - direct).astype(BF16)

    for jc in chips_of(phases[0]):
        kernel_tile(jc)
        for j in (2 * jc + 1, 2 * jc):
            last_copy(j).start()
    for jc in chips_of(phases[1]):
        kernel_tile(jc)
    for j in peers_of(phases[0]):
        last_copy(j).wait_send()
    for j in peers_of(phases[1]):
        last_copy(j).start()
        later(last_copy(j).wait_send)
    own = aligned(s, CAP)
    returned[own, :] = kernel_out[own, :]

    for phase in range(2):
        for j in peers_of(phases[phase]):
            last_copy(j).wait_recv()

        def add_rows(b, phase=phase):
            rows = aligned(b, tile)
            start[rows, :] += sum(
                dot(gather_mat[rows, source_rows(i)], returned[source_rows(i), :])
                for i in phases[phase]
            )

        loop(0, OWN // tile, add_rows)

    def fold(b, sums):
        rows = aligned(b, tile)
        cur = current[rows, :].astype(F32)
        return (
            sums[0] + jnp.sum(cur * start[rows, :], axis=0, keepdims=True),
            sums[1] + jnp.sum(cur * cur, axis=0, keepdims=True),
        )

    none = jnp.zeros((1, NV), F32)
    cross, square = lax.fori_loop(0, OWN // tile, fold, (none, none))

    def ratio(above, below):
        return above / jnp.where(below == 0.0, 1.0, below)

    local = ratio(cross, square)

    def fold_rest(b, acc):
        rows = aligned(b, tile)
        rest = start[rows, :] - local * current[rows, :].astype(F32)
        return acc + jnp.sum(rest * rest, axis=0, keepdims=True)

    rest_sq = lax.fori_loop(0, OWN // tile, fold_rest, none)

    def combine(read, count):
        cross = sum(read(i)[0:1] for i in range(count))
        square = sum(read(i)[1:2] for i in range(count))
        alpha = ratio(cross, square)
        rest = none
        for i in range(count):
            item = read(i)
            apart = ratio(item[0:1], item[1:2]) - alpha
            rest = rest + (item[2:3] + apart * apart * item[1:2])
        return cross, square, rest

    stats_mine[...] = jnp.concatenate([cross, square, rest_sq] + [none] * 5, axis=0)

    def stat_copy(j):
        return remote(
            stats_mine, stats_in.at[s], stat_send.at[j], stat_recv.at[j], g, peers_at[j]
        )

    def stat_ring_copy(k):
        return remote(
            stats_group,
            stats_all.at[g],
            stat_ring_send.at[k],
            stat_ring_recv.at[k],
            rings_at[k],
            s,
        )

    for j in range(1, B):
        stat_copy(j).start()
        later(stat_copy(j).wait_send)
    stats_in[s] = stats_mine[...]
    for j in range(1, B):
        stat_copy(j).wait_recv()
    stats_group[...] = jnp.concatenate(
        list(combine(lambda i: stats_in[i], B)) + [none] * 5, axis=0
    )
    for k in range(1, KR):
        stat_ring_copy(k).start()
        later(stat_ring_copy(k).wait_send)
    stats_all[g] = stats_group[...]
    for k in range(1, KR):
        stat_ring_copy(k).wait_recv()
    cross, square, rest_sq = combine(lambda i: stats_all[i], KR)

    alpha = cross / square
    beta = jnp.sqrt(rest_sq / rows_total + epsilon_mean)
    lanczos[...] = jnp.concatenate([alpha, beta] + [none] * 6, axis=0)

    drain()


def finish(start_ref, current_ref, lanczos_ref, next_ref, alpha_ref, beta_ref):
    alpha = lanczos_ref[0:1, :]
    beta = lanczos_ref[1:2, :]
    next_ref[...] = ((start_ref[...] - alpha * current_ref[...].astype(F32)) / beta).astype(BF16)
    alpha_ref[...] = alpha
    beta_ref[...] = beta


def per_device(
    planes,
    current,
    previous,
    energies,
    targets,
    layer_ids,
    conduction_pairs,
    valence_pairs,
    exchange_pairs,
    screened,
    coulomb,
    beta_prev,
):
    KR, B = lax.axis_size("kring"), lax.axis_size("band")
    OWN, NV = current.shape
    SLOT, NG = conduction_pairs.shape
    CAP = SLOT // B
    NB = B // 2
    NH = NV // 2
    GC = NG // NB
    GD = NG // B
    CH = SLOT // planes
    KY = KR // 2
    GY = NG // KY
    NQ = B
    NE = NH // NQ
    LANE = min(128, NH)
    GL = min(128, NG)
    J = NG // GL
    by_rows = jnp.transpose(screened.reshape(KR, 2, GD, 2, J, GL), (0, 1, 2, 4, 3, 5)).reshape(
        2 * KR, GD * J * 2, GL
    )
    vmem = pltpu.VMEM
    dma = pltpu.SemaphoreType.DMA
    scratch = [
        vmem((OWN, NV), BF16),
        vmem((OWN, NV), BF16),
        vmem((SLOT, NG), BF16),
        vmem((SLOT, NG), BF16),
        vmem((2, GD * J * 2, GL), BF16),
        vmem((2, KR * 2, 2, GD, NG), BF16),
        vmem((B, CAP, NV), BF16),
        vmem((SLOT, NV), BF16),
        vmem((planes, 2 * NV, CH), BF16),
        vmem((OWN, SLOT), BF16),
        vmem((1, OWN), F32),
        vmem((1, SLOT), F32),
        vmem((OWN, LANE), F32),
        vmem((SLOT, LANE), F32),
        vmem((OWN, LANE), F32),
        vmem((2, NV, NG), F32),
        vmem((2, NV, NG), F32),
        vmem((2, 2, NH, NG), F32),
        vmem((2, NB, 2, NH, GC), BF16),
        vmem((2, NB, 2, NH, GC), BF16),
        vmem((KY, 2, NH, GY), BF16),
        vmem((KY, 2, NH, GY), BF16),
        vmem((NH, 2 * GC), BF16),
        vmem((NH, KR * 2 * GC), BF16),
        vmem((2, NH, NG), F32),
        vmem((2, NH, GY), F32),
        vmem((NQ, 2, NE, GY), F32),
        vmem((2, NE, GY), F32),
        vmem((2, NH, GY), F32),
        vmem((2, GY, NH), BF16),
        vmem((2, GC, NH), BF16),
        vmem((2, NG, NV), BF16),
        vmem((2, NG, NV), BF16),
        vmem((SLOT, NV), F32),
        vmem((SLOT, NV), BF16),
        vmem((SLOT, NV), BF16),
        vmem((8, NV), F32),
        vmem((B, 8, NV), F32),
        vmem((8, NV), F32),
        vmem((KR, 8, NV), F32),
        dma((5,)),
        dma((2,)),
        dma((B,)),
        dma((B,)),
        dma((2, planes)),
        dma((2, planes)),
        dma((2, NB)),
        dma((2, NB)),
        dma,
        dma,
        dma((KR,)),
        dma((KR,)),
        dma((2, KY)),
        dma((2, KY)),
        dma((2, NQ)),
        dma((2, NQ)),
        dma((KY,)),
        dma((KY,)),
        dma((NB,)),
        dma((NB,)),
        dma((NB,)),
        dma((NB,)),
        dma((B,)),
        dma((B,)),
        dma((B,)),
        dma((B,)),
        dma((KR,)),
        dma((KR,)),
    ]
    in_vmem = pl.BlockSpec(memory_space=pltpu.VMEM)
    in_hbm = pl.BlockSpec(memory_space=pl.ANY)
    start, lanczos = pl.pallas_call(
        functools.partial(kernel, (KR, B, planes, CAP, OWN, SLOT, NG, NV)),
        out_shape=(
            jax.ShapeDtypeStruct((OWN, NV), F32),
            jax.ShapeDtypeStruct((8, NV), F32),
        ),
        in_specs=[in_vmem] * 5 + [in_hbm] * 6,
        out_specs=(in_vmem, in_vmem),
        scratch_shapes=scratch,
        compiler_params=pltpu.CompilerParams(
            collective_id=0, has_side_effects=True, vmem_limit_bytes=62 * 1024 * 1024
        ),
    )(
        targets.reshape(1, OWN),
        layer_ids.reshape(SLOT // LANE, LANE),
        energies.reshape(1, OWN),
        coulomb,
        beta_prev.reshape(1, NV),
        current,
        previous,
        conduction_pairs,
        valence_pairs,
        exchange_pairs,
        by_rows,
    )
    rows = OWN // 4
    next_vector, alpha, beta = pl.pallas_call(
        finish,
        grid=(4,),
        out_shape=(
            jax.ShapeDtypeStruct((OWN, NV), BF16),
            jax.ShapeDtypeStruct((1, NV), F32),
            jax.ShapeDtypeStruct((1, NV), F32),
        ),
        in_specs=[
            pl.BlockSpec((rows, NV), lambda b: (b, 0)),
            pl.BlockSpec((rows, NV), lambda b: (b, 0)),
            pl.BlockSpec((8, NV), lambda b: (0, 0)),
        ],
        out_specs=(
            pl.BlockSpec((rows, NV), lambda b: (b, 0)),
            pl.BlockSpec((1, NV), lambda b: (0, 0)),
            pl.BlockSpec((1, NV), lambda b: (0, 0)),
        ),
    )(start, current, lanczos)
    return next_vector, alpha.reshape(NV), beta.reshape(NV)


def solution(mesh):
    in_specs = (
        P(("kring", "band"), None),
        P(("kring", "band"), None),
        P(("kring", "band")),
        P(("kring", "band")),
        P(("kring", "band")),
        P(("kring", "band"), None),
        P(("kring", "band"), None),
        P(("kring", "band"), None),
        P(None, None, "band", None, None),
        P(),
        P(),
    )
    out_specs = (P(("kring", "band"), None), P(), P())
    planes = max(2, mesh.shape["band"] // 4)
    return jax.shard_map(
        functools.partial(per_device, planes),
        mesh=mesh,
        in_specs=in_specs,
        out_specs=out_specs,
        check_vma=False,
    )
```

time: 133 us -> 131 us (0.985)
  local copies, waits for them, and re-layouts: 12.9 us -> 0 us
  Pallas kernels: 120 us -> 130 us
    pallas_call x1, Pallas kernels: 120 us -> 126 us  [per_device(): pl.pallas_call(functools.partial(kernel, (KR, B, planes, CAP, OWN, SLOT,...]
    transpose x1 -> x0, local copies, waits for them, and re-layouts: 5.48 us -> none  [per_device(): jnp.transpose(screened, (3, 0, 1, 2, 4)).reshape(2, KR * 2 * GD, NG)]
    unnamed x3 -> x0, local copies, waits for them, and re-layouts: 4.74 us -> none
    pallas_call x0 -> x1, Pallas kernels: none -> 3.86 us  [per_device(): pl.pallas_call(finish, grid=(4,), out_shape=(jax.ShapeDtypeStruct((OWN, N...]
    reshape x2 -> x0, local copies, waits for them, and re-layouts: 2.65 us -> none  [the longest x1 1.34 us: per_device(): coulomb.reshape(4, NG)]
where the time goes in v2:
time: 131 us; the launch traced here: 130 us
  Pallas kernels  130 us (99%)
    pallas_call x1, Pallas kernels, per_device(): pl.pallas_call(functools.partial(kernel, (KR, B, planes, CAP, OWN, SLOT,...  126 us
    pallas_call x1, Pallas kernels, per_device(): pl.pallas_call(finish, grid=(4,), out_shape=(jax.ShapeDtypeStruct((OWN, N...  3.86 us

profile of v2, /device:TPU:1, one launch (start us, length us, event | category | flops | bytes accessed | tf_op | source)
XLA Modules:
  0.0 130.4 jit_solution(4680895015581533150)
XLA Ops:
  0.6 125.9 %shard_map.130 = (f32[2048,256]{1,0:T(8,128)}, f32[8,256]{1,0:T(8,128)}) custom-call(s32[1,2048]{1,0:T(1,128)} %bitcast.13, s32[20,128]{1,0:T(8,128)} %bitcast.12, f32[1,2048]{1,0:T(1,128)} %bitcast.14, f32[2,2,1024]{2,1,0:T(2,128)} %coulomb_ref.1, f32[1,256]{1,0:T(1,128)} %bitcast.15, bf16[2048,256]{1,0:T(8,128)(2,1)} %current_ref.1, ...), custom_call_target="tpu_custom_call" | custom-call | tf_op jit(solution)/shard_map/pallas_call | solution.py:834
  126.5 3.9 %shard_map.131 = (bf16[2048,256]{1,0:T(8,128)(2,1)}, f32[1,256]{1,0:T(1,128)}, f32[1,256]{1,0:T(1,128)}) custom-call(f32[2048,256]{1,0:T(8,128)} %get-tuple-element.8.start_ref, bf16[2048,256]{1,0:T(8,128)(2,1)} %current_ref.1, f32[8,256]{1,0:T(8,128)} %get-tuple-element.9.lanczos_ref), custom_call_target="tpu_custom_call" | custom-call | tf_op jit(solution)/shard_map/pallas_call | solution.py:860

commit v3 on v2

--- a/solution.py
+++ b/solution.py
@@ -287,12 +287,14 @@
                     rows[jh * PB : (jh + 1) * PB]
                 )
 
-    loop(0, 2 * KR, part)
+    first_part = KR + KR // 4
+    loop(0, first_part, part)
     for j in peers_of(phases[0]):
         first_copy(j).wait_send()
     for j in peers_of(phases[1]):
         first_copy(j).start()
         later(first_copy(j).wait_send)
+    loop(first_part, 2 * KR, part)
     shared = screened.at[:, :, core]
     share = remote(shared, shared, share_send, share_recv, g, partner)
     share.start()
@@ -493,22 +495,6 @@
     for q in range(1, NQ):
         over_layer(q).start()
         later(over_layer(q).wait_send)
-    build_gather()
-    layer_total = total_part[:, aligned(layer_here, NE), :]
-    for q in range(1, NQ):
-        over_layer(q).wait_recv()
-        layer_total = layer_total + total_in[q]
-    quarter = aligned(ring_y, GY)
-    for layer in range(2):
-        coupled_part[layer] = (
-            coulomb_ref[layer, 0:1, quarter] * layer_total[0]
-            + coulomb_ref[layer, 1:2, quarter] * layer_total[1]
-        )
-    for q in range(1, NQ):
-        coupled_copy(q).start()
-        later(coupled_copy(q).wait_send)
-    coupled_t[:, aligned(layer_here, NE), :] = coupled_part[...]
-
     fetches[4].start()
     share.wait_recv()
     for k in range(1, KR):
@@ -522,6 +508,21 @@
         for jc in range((i + 1) * NX - 1, max(i * NX - 1, 0), -1):
             send_part(1, jc, direct_part(1, part_x, jc))
 
+    layer_total = total_part[:, aligned(layer_here, NE), :]
+    for q in range(1, NQ):
+        over_layer(q).wait_recv()
+        layer_total = layer_total + total_in[q]
+    quarter = aligned(ring_y, GY)
+    for layer in range(2):
+        coupled_part[layer] = (
+            coulomb_ref[layer, 0:1, quarter] * layer_total[0]
+            + coulomb_ref[layer, 1:2, quarter] * layer_total[1]
+        )
+    for q in range(1, NQ):
+        coupled_copy(q).start()
+        later(coupled_copy(q).wait_send)
+    coupled_t[:, aligned(layer_here, NE), :] = coupled_part[...]
+
     def y_copy(t):
         return remote(
             coupled_tile,
@@ -548,7 +549,6 @@
     coupled_all[:, quarter, mine] = coupled_tile[...]
     coupled_forward(0).start()
     later(coupled_forward(0).wait_send)
-    build_start()
 
     def gather_copy(jc):
         return remote(
@@ -627,6 +627,9 @@
         later(last_copy(j).wait_send)
     own = aligned(s, CAP)
     returned[own, :] = kernel_out[own, :]
+
+    build_gather()
+    build_start()
 
     for phase in range(2):
         for j in peers_of(phases[phase]):

time: 131 us -> 127 us (0.969)
  Pallas kernels: 130 us -> 126 us
    pallas_call x1, Pallas kernels: 126 us -> 122 us  [per_device(): pl.pallas_call(functools.partial(kernel, (KR, B, planes, CAP, OWN, SLOT,...]
where the time goes in v3:
time: 127 us; the launch traced here: 126 us
  Pallas kernels  126 us (99%)
    pallas_call x1, Pallas kernels, per_device(): pl.pallas_call(functools.partial(kernel, (KR, B, planes, CAP, OWN, SLOT,...  122 us
    pallas_call x1, Pallas kernels, per_device(): pl.pallas_call(finish, grid=(4,), out_shape=(jax.ShapeDtypeStruct((OWN, N...  3.86 us

profile of v3, /device:TPU:1, one launch (start us, length us, event | category | flops | bytes accessed | tf_op | source)
XLA Modules:
  0.0 126.2 jit_solution(4628478901181024948)
XLA Ops:
  0.6 121.7 %shard_map.130 = (f32[2048,256]{1,0:T(8,128)}, f32[8,256]{1,0:T(8,128)}) custom-call(s32[1,2048]{1,0:T(1,128)} %bitcast.13, s32[20,128]{1,0:T(8,128)} %bitcast.12, f32[1,2048]{1,0:T(1,128)} %bitcast.14, f32[2,2,1024]{2,1,0:T(2,128)} %coulomb_ref.1, f32[1,256]{1,0:T(1,128)} %bitcast.15, bf16[2048,256]{1,0:T(8,128)(2,1)} %current_ref.1, ...), custom_call_target="tpu_custom_call" | custom-call | tf_op jit(solution)/shard_map/pallas_call | solution.py:837
  122.4 3.9 %shard_map.131 = (bf16[2048,256]{1,0:T(8,128)(2,1)}, f32[1,256]{1,0:T(1,128)}, f32[1,256]{1,0:T(1,128)}) custom-call(f32[2048,256]{1,0:T(8,128)} %get-tuple-element.8.start_ref, bf16[2048,256]{1,0:T(8,128)(2,1)} %current_ref.1, f32[8,256]{1,0:T(8,128)} %get-tuple-element.9.lanczos_ref), custom_call_target="tpu_custom_call" | custom-call | tf_op jit(solution)/shard_map/pallas_call | solution.py:863
